TPU v7x, 32 devices: a whole 2x2x4 slice. The times are simulated.
32 devices in a mesh: enc: 4 (over y, x), dec: 4 (over z), ret: 2 (over core).
Axes of the slice: x: 2, y: 2, z: 4, core: 2. Of those that a mesh axis runs over, the one named last changes fastest.
Arguments:
- enc_states: bfloat16 [8, 2, 256, 4096], P('enc', 'ret'), may hold values from -22 to 22
- kv_weight: bfloat16 [4096, 64, 128], P(None, 'dec'), may hold values from -1 to 1
- queries: bfloat16 [2, 128, 64, 64], P('ret', None, ('dec', 'enc')), may hold values from -47 to 47
- out_grad: bfloat16 [2, 128, 64, 64], P('ret', None, ('dec', 'enc')), may hold values from -6 to 6
- passage_order: int32 [2, 8], P('ret'), may hold values from 0 to 7, each once within a row
- passage_blocks: int32 [2, 8], P('ret'), may hold values from 1 to 2
- ret_tokens: bfloat16 [8, 2, 256, 768], P('enc', 'ret'), may hold values from -6 to 6
- ret_weight: bfloat16 [768, 768], replicated, may hold values from -0.21875 to 0.21875
- question_emb: float32 [2, 768], P('ret'), may hold values from -7 to 7
Outputs:
- kv_grad: bfloat16 [8, 2, 256, 64, 128], P('enc', 'ret', None, 'dec')
- kv_weight_grad: bfloat16 [4096, 64, 128], P(('enc', 'ret'), 'dec')
- ret_weight_grad: bfloat16 [768, 768], replicated
Inputs may be any that keep to these rules, and one draw needn't show every extreme that they name: `passage_order`: each row lists every passage of its group once; slots i * 8 to (i + 1) * 8 - 1 belong to question i of the group.
All inputs are finite; a program needn't handle non-finite values.
Results may differ from a plain program's by a relative error of at most 0.025.
Values may be sent and summed in bfloat16 or wider, within the bound.
A program may use at most 128 MiB of HBM per device.

v0:
```python
import math
import jax
import jax.numpy as jnp
from jax import lax
from jax.sharding import PartitionSpec as P

HEADS = 64
BLK = 128
PASS = 8


def gelu_grad(pre_act, upstream):
    return jax.vjp(jax.nn.gelu, pre_act)[1](upstream)[0]


def on_device(
    enc_states,
    kv_weight,
    queries,
    out_grad,
    passage_order,
    passage_blocks,
    ret_tokens,
    ret_weight,
    question_emb,
):
    pass_dev = enc_states.shape[0]
    slot_len = enc_states.shape[2]
    width = enc_states.shape[3]
    heads_dec = kv_weight.shape[1]
    pair_width = kv_weight.shape[2]
    head_dim = pair_width // 2
    enc_rank = lax.axis_index("enc")
    dec_rank = lax.axis_index("dec")
    order_row = passage_order[0]
    blocks_row = passage_blocks[0]
    group_pass = order_row.shape[0]
    question_count = queries.shape[0]
    query_len = queries.shape[1]
    highest = lax.Precision.HIGHEST
    own_blocks = lax.dynamic_slice_in_dim(blocks_row, enc_rank * pass_dev, pass_dev)
    tok_rows = enc_states.reshape(pass_dev * slot_len, width)
    weight_flat = kv_weight.reshape(width, heads_dec * pair_width)
    key_value = jnp.dot(tok_rows, weight_flat, preferred_element_type=jnp.float32)
    key_value = key_value.reshape(pass_dev * slot_len, heads_dec, pair_width)
    gathered = lax.all_to_all(key_value, "enc", split_axis=1, concat_axis=0, tiled=True)
    heads_here = gathered.shape[1]
    gathered = gathered.reshape(group_pass, slot_len, heads_here, pair_width)
    chosen = order_row.reshape(question_count, PASS)
    key_count = PASS * slot_len
    selected = gathered[chosen].reshape(question_count, key_count, heads_here, pair_width)
    keys = selected[..., :head_dim]
    values = selected[..., head_dim:]
    positions = jnp.arange(slot_len, dtype=jnp.int32)
    live = (positions[None, None, :] < BLK * blocks_row[chosen][:, :, None]).reshape(
        question_count, key_count
    )
    scale = 1.0 / math.sqrt(head_dim)
    query_wide = queries.astype(jnp.float32)
    grad_wide = out_grad.astype(jnp.float32)
    scores = jnp.einsum("qlhc,qkhc->qhlk", query_wide, keys, precision=highest) * scale
    masked = jnp.where(live[:, None, None, :], scores, -1e30)
    top = jnp.max(masked, axis=-1, keepdims=True)
    expo = jnp.where(live[:, None, None, :], jnp.exp(masked - top), 0.0)
    probs = expo / jnp.sum(expo, axis=-1, keepdims=True)
    probs_low = probs.astype(jnp.bfloat16)
    attended = jnp.einsum(
        "qhlk,qkhc->qlhc", probs_low.astype(jnp.float32), values, precision=highest
    )
    value_grad = jnp.einsum(
        "qhlk,qlhc->qkhc", probs_low, out_grad, preferred_element_type=jnp.float32
    )
    prob_grad = jnp.einsum("qlhc,qkhc->qhlk", grad_wide, values, precision=highest)
    row_dot = jnp.einsum("qlhc,qlhc->qhl", grad_wide, attended)
    score_grad = (probs * (prob_grad - row_dot[..., None]) * scale).astype(jnp.bfloat16)
    key_grad = jnp.einsum(
        "qhlk,qlhc->qkhc", score_grad, queries, preferred_element_type=jnp.float32
    )
    pair_grad = jnp.concatenate([key_grad, value_grad], axis=-1).astype(jnp.bfloat16)
    pair_grad = pair_grad.reshape(question_count * PASS, slot_len, heads_here, pair_width)
    placed = (
        jnp.zeros((group_pass, slot_len, heads_here, pair_width), jnp.bfloat16)
        .at[order_row]
        .set(pair_grad)
    )
    returned = lax.all_to_all(
        placed.reshape(group_pass * slot_len, heads_here, pair_width),
        "enc",
        split_axis=0,
        concat_axis=1,
        tiled=True,
    )
    kv_grad = returned.reshape(pass_dev, 1, slot_len, heads_dec, pair_width)
    mass_part = jnp.sum(probs, axis=(1, 2)).reshape(question_count, PASS, slot_len).sum(axis=-1) / (
        HEADS * query_len
    )
    ret_rows = ret_tokens.reshape(pass_dev * slot_len, ret_tokens.shape[3])
    ret_width = ret_rows.shape[1]
    pre_act = jnp.dot(ret_rows, ret_weight, preferred_element_type=jnp.float32).reshape(
        pass_dev, slot_len, ret_width
    )
    hidden = jax.nn.gelu(pre_act)
    own_live = positions[None, :] < BLK * own_blocks[:, None]
    own_length = (BLK * own_blocks).astype(jnp.float32)
    embed_own = jnp.sum(jnp.where(own_live[..., None], hidden, 0.0), axis=1) / own_length[:, None]
    owner_map = (
        order_row[:, None] == enc_rank * pass_dev + jnp.arange(pass_dev, dtype=jnp.int32)[None, :]
    ).astype(jnp.float32)
    slot_embed = jnp.dot(owner_map, embed_own, precision=highest)
    emb_rep = jnp.repeat(question_emb, PASS, axis=0)
    score_part = jnp.sum(emb_rep * slot_embed, axis=-1) * (dec_rank == 0).astype(jnp.float32)
    passage_mass, ret_scores = lax.psum(
        (mass_part, score_part.reshape(question_count, PASS)), ("enc", "dec")
    )
    top_score = jnp.max(ret_scores, axis=-1, keepdims=True)
    expo_score = jnp.exp(ret_scores - top_score)
    score_gap = expo_score / jnp.sum(expo_score, axis=-1, keepdims=True) - passage_mass
    gap_rows = score_gap.reshape(-1, 1) * emb_rep
    embed_grad = jnp.dot(jnp.transpose(owner_map), gap_rows, precision=highest)
    hidden_grad = jnp.where(
        own_live[..., None], (embed_grad / own_length[:, None])[:, None, :], 0.0
    )
    pre_grad = gelu_grad(pre_act, hidden_grad).astype(jnp.bfloat16)
    ret_part_grad = lax.dot_general(
        ret_rows,
        pre_grad.reshape(-1, ret_width),
        (((0,), (0,)), ((), ())),
        preferred_element_type=jnp.float32,
    )
    ret_weight_grad = lax.psum(ret_part_grad.astype(jnp.bfloat16), ("enc", "ret"))
    grad_flat = returned.reshape(pass_dev * slot_len, heads_dec * pair_width)
    term = lax.dot_general(
        tok_rows, grad_flat, (((0,), (0,)), ((), ())), preferred_element_type=jnp.float32
    )
    weight_total = lax.psum_scatter(
        term.reshape(
            width // (lax.axis_size("enc") * lax.axis_size("ret")) * lax.axis_size(("enc", "ret")),
            heads_dec,
            pair_width,
        ).astype(jnp.bfloat16),
        ("enc", "ret"),
        scatter_dimension=0,
        tiled=True,
    )
    return (kv_grad, weight_total, ret_weight_grad)


def solution(mesh):
    return jax.shard_map(
        on_device,
        mesh=mesh,
        in_specs=(
            P("enc", "ret", None, None),
            P(None, "dec", None),
            P("ret", None, ("dec", "enc"), None),
            P("ret", None, ("dec", "enc"), None),
            P("ret", None),
            P("ret", None),
            P("enc", "ret", None, None),
            P(),
            P("ret", None),
        ),
        out_specs=(P("enc", "ret", None, "dec", None), P(("enc", "ret"), "dec", None), P()),
        check_vma=False,
    )
```

profile of v0, /device:TPU:0, one launch (start us, length us, event | category | flops | bytes accessed | tf_op | source)
XLA Modules:
  0.0 412.8 jit_solution(12834699166763895516)
XLA Ops:
  7.2 0.0 copy-start
  7.2 17.3 %copy.95 = bf16[512,8,16,128]{3,1,2,0:T(8,128)(2,1)} copy(bf16[512,8,16,128]{3,2,1,0:T(8,128)(2,1)} %bitcast.155) | data formatting | bytes 33554432
  24.5 20.7 %copy.64 = bf16[2048,4096]{1,0:T(8,128)(2,1)} copy(bf16[2048,4096]{0,1:T(8,128)(2,1)} %bitcast.152) | data formatting | bytes 33554432 | tf_op jit(solution)/shard_map/dot_general | solution.py:44
  45.3 14.2 %fusion.57 = f32[512,16,128]{2,0,1:T(8,128)} fusion(bf16[512,4096,1]{1,0,2:T(8,128)(2,1)} %bitcast.169, bf16[16,128,4096]{2,1,0:T(8,128)(2,1)} %bitcast.156), kind=kOutput, calls=%fused_computation.90 | convolution fusion | flops 8589934592 | bytes 25165824 | tf_op jit(solution)/shard_map/dot_general | solution.py:44
  59.4 0.0 copy-start.8
  59.4 5.3 %all-to-all-start = ((f32[512,16,128]{2,0,1:T(8,128)}), f32[512,16,128]{2,0,1:T(8,128)}, u32[]{:S(2)}, u32[]{:S(2)}) async-start(f32[512,16,128]{2,0,1:T(8,128)} %fusion.57), calls=%async_computation | async-start | bytes 8388608 | tf_op jit(solution)/shard_map/all_to_all | solution.py:46
  64.8 0.0 copy-done.7
  64.9 0.6 gather_fusion
  65.5 0.1 lt.61
  65.6 0.1 fusion.55
  65.7 0.1 iota_compare_fusion
  65.8 2.2 select_reduce_fusion
  68.0 0.3 fusion.29
  68.3 45.3 %all-to-all-done = f32[512,16,128]{2,0,1:T(8,128)} async-done(((f32[512,16,128]{2,0,1:T(8,128)}), f32[512,16,128]{2,0,1:T(8,128)}, u32[]{:S(2)}, u32[]{:S(2)}) %all-to-all-start) | async-done | bytes 4194336 | tf_op jit(solution)/shard_map/all_to_all | solution.py:46
  113.6 2.5 copy.65
  116.1 2.3 copy.66
  118.3 4.9 %gather_fusion.1 = f32[8,256,4,128]{3,1,2,0:T(8,128)} fusion(f32[8,256,4,128]{3,1,2,0:T(8,128)} %copy.66, s32[1024]{0:T(1024)S(1)} %pad_clamp_fusion), kind=kCustom, calls=%fused_computation.1 | custom fusion | bytes 8388640 | tf_op jit(solution)/shard_map/gather | solution.py:51
  123.3 5.4 %copy.67 = f32[8,256,4,128]{1,0,3,2:T(8,128)} copy(f32[8,256,4,128]{3,1,2,0:T(8,128)} %gather_fusion.1) | data formatting | bytes 8388608 | tf_op jit(solution)/shard_map/gather | solution.py:51
  128.7 4.9 %reshape.262 = f32[1,2048,4,128]{1,3,2,0:T(8,128)} reshape(f32[8,256,4,128]{1,0,3,2:T(8,128)} %copy.67) | data formatting | bytes 8388608 | tf_op jit(solution)/shard_map/reshape | solution.py:51
  133.6 0.0 copy-done.6
  133.6 5.1 %fusion.8 = f32[4,2048,128]{2,1,0:T(8,128)S(1)} fusion(f32[1,2048,4,128]{1,3,2,0:T(8,128)} %reshape.262, bf16[1,128,4,64]{1,3,2,0:T(8,128)(2,1)S(1)} %copy-done.6), kind=kOutput, calls=%fused_computation.23 | convolution fusion | flops 805306368 | bytes 6356992 | tf_op jit(solution)/shard_map/qlhc,qkhc->qhlk/dot_general | solution.py:61
  138.7 0.0 copy-start.3
  138.7 0.0 copy-start.9
  138.7 1.6 fusion.56
  140.3 0.0 copy-start.4
  140.3 0.6 copy-done.3
  140.9 1.4 fusion.28
  142.2 1.8 convolution_convert_fusion.1
  144.1 4.0 fusion.2
  148.1 0.8 convolution_convert_fusion.2
  149.0 1.3 copy.92
  150.2 2.2 copy.71
  152.4 1.5 copy.93
  153.9 2.0 copy.72
  155.9 4.1 pad_maximum_fusion
  160.0 0.5 broadcast_in_dim.72
  160.5 3.3 scatter_fusion
  163.8 0.1 copy.73
  164.0 10.7 %copy.74 = bf16[2048,4,128]{2,1,0:T(4,128)(2,1)} copy(bf16[2048,4,128]{2,0,1:T(8,128)(2,1)S(1)} %bitcast.159) | data formatting | bytes 4194304 | tf_op jit(solution)/shard_map/reshape | solution.py:87
  174.7 4.4 %all-to-all-start.1 = ((bf16[2048,4,128]{2,1,0:T(4,128)(2,1)}), bf16[2048,4,128]{2,1,0:T(4,128)(2,1)}, u32[]{:S(2)}, u32[]{:S(2)}) async-start(bf16[2048,4,128]{2,1,0:T(4,128)(2,1)} %copy.74), calls=%async_computation.1 | async-start | bytes 4194304 | tf_op jit(solution)/shard_map/all_to_all | solution.py:86
  179.1 0.0 all-reduce.3.cloned.1.call-start
  179.2 2.7 fusion.54
  181.9 0.1 reduce_sum.59
  182.0 42.9 %all-reduce = (f32[1,8]{1,0:T(1,128)S(1)}, f32[1,8]{1,0:T(1,128)S(1)}) all-reduce(f32[1,8]{1,0:T(1,128)S(1)} %get-tuple-element.26, f32[1,8]{1,0:T(1,128)S(1)} %get-tuple-element.27), channel_id=1, replica_groups=mesh['enc'=4,'dec'=4,'ret'=2] {'enc','dec'}, use_global_device_ids=true, to_apply=%region_11.12 | all-reduce | flops 16 | bytes 128 | tf_op jit(solution)/shard_map/psum | solution.py:112
  224.9 0.6 reduce_max.19
  225.5 1.3 fusion.53
  226.8 1.3 fusion.50
  228.1 0.3 convolution_divide_fusion
  228.3 1.2 fusion.19
  229.5 3.0 fusion.23
  232.5 0.0 all-reduce.3.cloned.1.call-update
  232.5 0.3 reduce-scatter.2.cloned.1.call-start
  232.8 0.0 all-to-all-done.1
  232.8 1.9 copy.75
  234.7 2.3 copy.77
  237.0 14.8 %convolution_convert_fusion = bf16[2048,4096]{1,0:T(8,128)(2,1)} fusion(bf16[512,2048]{0,1:T(8,128)(2,1)} %bitcast.164, bf16[512,4096]{1,0:T(8,128)(2,1)} %bitcast.170), kind=kOutput, calls=%fused_computation.5 | convolution fusion | flops 8598323200 | bytes 23068672 | tf_op jit(solution)/shard_map/dot_general | solution.py:132
  251.8 22.3 %copy.78 = bf16[4096,16,128]{2,1,0:T(8,128)(2,1)} copy(bf16[4096,16,128]{0,2,1:T(8,128)(2,1)} %bitcast.157) | data formatting | bytes 33554432 | tf_op jit(solution)/shard_map/convert_element_type | solution.py:140
  274.2 0.0 reduce-scatter.2.cloned.1.call-update
  274.2 12.1 %all-reduce.3.cloned.1.call-done = bf16[768,768]{0,1:T(8,128)(2,1)} async-done(((bf16[768,768]{0,1:T(8,128)(2,1)}), bf16[768,768]{0,1:T(8,128)(2,1)}) %all-reduce.3.cloned.1.call-update) | async-done | bytes 1179664 | tf_op jit(solution)/shard_map/psum | solution.py:130
  286.3 2.4 copy.80
  288.7 0.1 copy.76
  288.9 0.0 copy-start.1
  288.9 2.7 copy.79
  291.5 114.4 %reduce-scatter.2.cloned.1.call-done = bf16[512,16,128]{2,1,0:T(8,128)(2,1)} async-done(((bf16[4096,16,128]{2,1,0:T(8,128)(2,1)}), bf16[512,16,128]{2,1,0:T(8,128)(2,1)}) %reduce-scatter.2.cloned.1.call-update) | async-done | bytes 2097168 | tf_op jit(solution)/shard_map/reduce_scatter | solution.py:135
  (24 shorter events, 0.1 us)
Async XLA Ops:
  7.2 58.6 %copy-start = (bf16[768,768]{1,0:T(8,128)(2,1)S(1)}, bf16[768,768]{1,0:T(8,128)(2,1)}, u32[]{:S(2)}) copy-start(bf16[768,768]{1,0:T(8,128)(2,1)} %param.16) | copy-start | bytes 3538948
  59.4 5.4 %copy-start.7 = (f32[1,768]{1,0:T(1,128)S(1)}, f32[1,768]{1,0:T(1,128)}, u32[]{:S(2)}) copy-start(f32[1,768]{1,0:T(1,128)} %param.17) | copy-start | bytes 9220
  59.4 5.4 %copy-start.10 = (s32[1,8]{1,0:T(1,128)S(1)}, s32[1,8]{1,0:T(1,128)}, u32[]{:S(2)}) copy-start(s32[1,8]{1,0:T(1,128)} %param.13) | copy-start | bytes 100
  59.4 5.4 %copy-start.2 = (s32[1,8]{1,0:T(1,128)S(1)}, s32[1,8]{1,0:T(1,128)}, u32[]{:S(2)}) copy-start(s32[1,8]{1,0:T(1,128)} %param.14) | copy-start | bytes 100
  59.4 6.4 %copy-start.8 = (bf16[2,1,256,768]{3,2,1,0:T(8,128)(2,1)S(1)}, bf16[2,1,256,768]{3,2,1,0:T(8,128)(2,1)}, u32[]{:S(2)}) copy-start(bf16[2,1,256,768]{3,2,1,0:T(8,128)(2,1)} %param.15) | copy-start | bytes 2359300
  59.4 54.1 %all-to-all-start = ((f32[512,16,128]{2,0,1:T(8,128)}), f32[512,16,128]{2,0,1:T(8,128)}, u32[]{:S(2)}, u32[]{:S(2)}) async-start(f32[512,16,128]{2,0,1:T(8,128)} %fusion.57), calls=%async_computation | async-start | bytes 8388608 | tf_op jit(solution)/shard_map/all_to_all | solution.py:46
  128.7 4.9 %copy-start.6 = (bf16[1,128,4,64]{1,3,2,0:T(8,128)(2,1)S(1)}, bf16[1,128,4,64]{1,3,2,0:T(8,128)(2,1)}, u32[]{:S(2)}) copy-start(bf16[1,128,4,64]{1,3,2,0:T(8,128)(2,1)} %param.11) | copy-start | bytes 196612
  138.7 2.2 copy-start.3
  138.7 2.2 copy-start.9
  140.3 3.8 copy-start.4
  174.7 58.1 %all-to-all-start.1 = ((bf16[2048,4,128]{2,1,0:T(4,128)(2,1)}), bf16[2048,4,128]{2,1,0:T(4,128)(2,1)}, u32[]{:S(2)}, u32[]{:S(2)}) async-start(bf16[2048,4,128]{2,1,0:T(4,128)(2,1)} %copy.74), calls=%async_computation.1 | async-start | bytes 4194304 | tf_op jit(solution)/shard_map/all_to_all | solution.py:86
  179.1 49.2 %copy-start.5 = (f32[2,256,768]{2,1,0:T(8,128)S(1)}, f32[2,256,768]{2,1,0:T(8,128)}, u32[]{:S(2)}) copy-start(f32[2,256,768]{2,1,0:T(8,128)} %get-tuple-element.25) | copy-start | bytes 4718596
  179.1 107.2 %all-reduce.3.cloned.1.call-start = ((), (), s32[]{:S(2)}) async-start(), calls=%async_computation.4 | async-start | bytes 2359296 | tf_op jit(solution)/shard_map/psum | solution.py:130
  232.5 173.5 %reduce-scatter.2.cloned.1.call-start = ((), (), s32[]{:S(2)}) async-start(), calls=%async_computation.3 | async-start | bytes 18874368 | tf_op jit(solution)/shard_map/reduce_scatter | solution.py:135
  288.9 117.1 %copy-start.1 = (bf16[768,768]{1,0:T(8,128)(2,1)S(1)}, bf16[768,768]{1,0:T(8,128)(2,1)}, u32[]{:S(2)}) copy-start(bf16[768,768]{1,0:T(8,128)(2,1)} %param.16) | copy-start | bytes 3538948
Sparse Core Ops, SparseCore 0:
  232.6 53.6 all-reduce.2
  290.5 115.4 reduce-scatter.1
where the time goes:
time: 415 us; the launch traced here: 413 us
  waiting for transfers between devices  172 us (41%)
  local copies, waits for them, and re-layouts  113 us (27%)
  matrix products  47.9 us (12%)
  blocking collectives  42.9 us (10%)
  between operations  14.3 us (3%)
  other arithmetic  12.9 us (3%)
  starting transfers between devices  10.1 us (2%)
    reduce_scatter x1, waiting for transfers between devices, on_device(): lax.psum_scatter(term.reshape(width // (lax.axis_size('enc') * lax.axis_s...  114 us
    all_to_all x1, waiting for transfers between devices, on_device(): lax.all_to_all(key_value, 'enc', split_axis=1, concat_axis=0, tiled=True)  45.3 us
    psum x1, blocking collectives, on_device(): lax.psum((mass_part, score_part.reshape(question_count, PASS)), ('enc', '...  42.9 us
    unnamed x29, local copies, waits for them, and re-layouts  25.9 us
    convert_element_type x1, local copies, waits for them, and re-layouts, on_device(): weight_total = lax.psum_scatter(term.reshape(width // (lax.axis_size('enc...  22.3 us
    dot_general x1, local copies, waits for them, and re-layouts, on_device(): jnp.dot(tok_rows, weight_flat, preferred_element_type=jnp.float32)  20.7 us
    dot_general x1, matrix products, on_device(): lax.dot_general(tok_rows, grad_flat, (((0,), (0,)), ((), ())), preferred_...  14.8 us
    dot_general x1, matrix products, on_device(): jnp.dot(tok_rows, weight_flat, preferred_element_type=jnp.float32)  14.2 us
  transfers between devices with their start and end apart: 4, of which 3 were waited for; matrix products, arithmetic and copies ran while one was open for 15% of the time, Pallas kernels for 0%

commit v1 on v0

--- a/solution.py
+++ b/solution.py
@@ -7,6 +7,18 @@
 HEADS = 64
 BLK = 128
 PASS = 8
+
+
+def cut_along(array, dim, size):
+    dims = array.shape
+    blocks = array.reshape(*dims[:dim], size, dims[dim] // size, *dims[dim + 1 :])
+    return jnp.moveaxis(blocks, dim, 0)
+
+
+def in_order(blocks, dim):
+    lengths = list(blocks.shape[1:])
+    lengths[dim] *= blocks.shape[0]
+    return jnp.moveaxis(blocks, 0, dim).reshape(lengths)
 
 
 def gelu_grad(pre_act, upstream):
@@ -43,7 +55,14 @@
     weight_flat = kv_weight.reshape(width, heads_dec * pair_width)
     key_value = jnp.dot(tok_rows, weight_flat, preferred_element_type=jnp.float32)
     key_value = key_value.reshape(pass_dev * slot_len, heads_dec, pair_width)
-    gathered = lax.all_to_all(key_value, "enc", split_axis=1, concat_axis=0, tiled=True)
+    size, index = (lax.axis_size("enc"), lax.axis_index("enc"))
+    blocks = cut_along(key_value, 1, size)
+    finished = [blocks[index]]
+    for lap in range(1, size):
+        sent = blocks[(index + lap) % size]
+        finished.append(lax.ppermute(sent, "enc", [(i, (i + lap) % size) for i in range(size)]))
+    blocks = jnp.stack(finished)[(index - jnp.arange(size)) % size]
+    gathered = in_order(blocks, 0)
     heads_here = gathered.shape[1]
     gathered = gathered.reshape(group_pass, slot_len, heads_here, pair_width)
     chosen = order_row.reshape(question_count, PASS)

time: 415 us -> 419 us (level)
  local copies, waits for them, and re-layouts: 113 us -> 120 us
  waiting for transfers between devices: 172 us -> 166 us
  other arithmetic: 12.9 us -> 17.1 us
    all_to_all x1 -> x0, waiting for transfers between devices: 45.3 us -> none  [on_device(): lax.all_to_all(key_value, 'enc', split_axis=1, concat_axis=0, tiled=True)]
    ppermute x0 -> x3, waiting for transfers between devices: none -> 39.6 us  [on_device(): lax.ppermute(sent, 'enc', [(i, (i + lap) % size) for i in range(size)])]
    gather x0 -> x2, local copies, waits for them, and re-layouts: none -> 7.45 us  [on_device(): blocks = jnp.stack(finished)[(index - jnp.arange(size)) % size]]
    ppermute x0 -> x3, starting transfers between devices: none -> 5.92 us  [on_device(): lax.ppermute(sent, 'enc', [(i, (i + lap) % size) for i in range(size)])]
    all_to_all x1 -> x0, starting transfers between devices: 5.33 us -> none  [on_device(): lax.all_to_all(key_value, 'enc', split_axis=1, concat_axis=0, tiled=True)]
    unnamed x29 -> x27, local copies, waits for them, and re-layouts: 25.9 us -> 25.9 us
  transfers between devices with their start and end apart: 4 -> 6, of which waited for: 3 -> 5; matrix products, arithmetic and copies ran while one was open for 15% -> 15% of each run, Pallas kernels for 0% -> 0%
where the time goes in v1:
time: 419 us; the launch traced here: 417 us
  waiting for transfers between devices  166 us (40%)
  local copies, waits for them, and re-layouts  120 us (29%)
  matrix products  46.9 us (11%)
  blocking collectives  43 us (10%)
  other arithmetic  17.1 us (4%)
  between operations  14.4 us (3%)
  starting transfers between devices  10.4 us (2%)
    reduce_scatter x1, waiting for transfers between devices, on_device(): lax.psum_scatter(term.reshape(width // (lax.axis_size('enc') * lax.axis_s...  114 us
    psum x1, blocking collectives, on_device(): lax.psum((mass_part, score_part.reshape(question_count, PASS)), ('enc', '...  43 us
    ppermute x3, waiting for transfers between devices, on_device(): lax.ppermute(sent, 'enc', [(i, (i + lap) % size) for i in range(size)])  39.6 us
    unnamed x27, local copies, waits for them, and re-layouts  25.9 us
    convert_element_type x1, local copies, waits for them, and re-layouts, on_device(): weight_total = lax.psum_scatter(term.reshape(width // (lax.axis_size('enc...  22.3 us
    dot_general x1, local copies, waits for them, and re-layouts, on_device(): jnp.dot(tok_rows, weight_flat, preferred_element_type=jnp.float32)  20.7 us
    dot_general x1, matrix products, on_device(): lax.dot_general(tok_rows, grad_flat, (((0,), (0,)), ((), ())), preferred_...  14.8 us
    dot_general x1, matrix products, on_device(): jnp.dot(tok_rows, weight_flat, preferred_element_type=jnp.float32)  12.3 us
  transfers between devices with their start and end apart: 6, of which 5 were waited for; matrix products, arithmetic and copies ran while one was open for 15% of the time, Pallas kernels for 0%

profile of v1, /device:TPU:0, one launch (start us, length us, event | category | flops | bytes accessed | tf_op | source)
XLA Modules:
  0.0 417.3 jit_solution(12259259670835769256)
XLA Ops:
  7.2 0.0 copy-start
  7.2 17.3 %copy.95 = bf16[512,8,16,128]{3,1,2,0:T(8,128)(2,1)} copy(bf16[512,8,16,128]{3,2,1,0:T(8,128)(2,1)} %bitcast.167) | data formatting | bytes 33554432
  24.6 20.7 %copy.63 = bf16[2048,4096]{1,0:T(8,128)(2,1)} copy(bf16[2048,4096]{0,1:T(8,128)(2,1)} %bitcast.164) | data formatting | bytes 33554432 | tf_op jit(solution)/shard_map/dot_general | solution.py:56
  45.3 12.3 %fusion.62 = f32[512,4,4,128]{3,0,2,1:T(8,128)S(1)} fusion(bf16[512,4096,1,1]{1,0,3,2:T(8,128)(2,1)} %bitcast.181, bf16[4,4,128,4096]{3,2,1,0:T(8,128)(2,1)} %bitcast.168), kind=kOutput, calls=%fused_computation.105 | convolution fusion | flops 8589934592 | bytes 25165824 | tf_op jit(solution)/shard_map/dot_general | solution.py:56
  57.6 0.0 copy-start.7
  57.6 1.6 dynamic-slice_bitcast_fusion.3
  59.3 3.0 collective-permute-start
  62.2 1.5 collective-permute-start.1
  63.7 1.4 collective-permute-start.2
  65.3 0.6 gather_fusion
  65.9 0.1 fusion.59
  66.0 0.1 lt.103
  66.1 0.1 iota_compare_fusion
  66.2 3.3 select_reduce_fusion
  69.5 0.3 fusion.29
  69.9 17.7 %collective-permute-done = f32[512,4,128]{2,0,1:T(8,128)} collective-permute-done((f32[512,4,128]{2,0,1:T(8,128)}, f32[512,4,128]{2,0,1:T(8,128)}, u32[]{:S(2)}, u32[]{:S(2)}) %collective-permute-start) | collective-permute-done | bytes 1048608 | tf_op jit(solution)/shard_map/ppermute | solution.py:63
  87.5 21.6 %collective-permute-done.1 = f32[512,4,128]{2,0,1:T(8,128)} collective-permute-done((f32[512,4,128]{2,0,1:T(8,128)}, f32[512,4,128]{2,0,1:T(8,128)}, u32[]{:S(2)}, u32[]{:S(2)}) %collective-permute-start.1) | collective-permute-done | bytes 1048608 | tf_op jit(solution)/shard_map/ppermute | solution.py:63
  109.1 0.3 collective-permute-done.2
  109.4 4.1 pad_maximum_fusion
  113.6 5.0 %gather_fusion.1 = f32[4,512,4,128]{3,1,2,0:T(8,128)} fusion(f32[4,512,4,128]{3,1,2,0:T(8,128)} %pad_maximum_fusion, s32[1024]{0:T(1024)S(1)} %pad_clamp_fusion), kind=kCustom, calls=%fused_computation.1 | custom fusion | bytes 8388624 | tf_op jit(solution)/shard_map/gather | solution.py:64
  118.5 2.5 copy.64
  121.0 2.3 copy.65
  123.3 4.9 %gather_fusion.2 = f32[8,256,4,128]{3,1,2,0:T(8,128)} fusion(f32[8,256,4,128]{3,1,2,0:T(8,128)} %copy.65, s32[1024]{0:T(1024)S(1)} %pad_clamp_fusion.1), kind=kCustom, calls=%fused_computation.2 | custom fusion | bytes 8388640 | tf_op jit(solution)/shard_map/gather | solution.py:70
  128.2 5.4 %copy.66 = f32[8,256,4,128]{1,0,3,2:T(8,128)} copy(f32[8,256,4,128]{3,1,2,0:T(8,128)} %gather_fusion.2) | data formatting | bytes 8388608 | tf_op jit(solution)/shard_map/gather | solution.py:70
  133.7 4.9 %reshape.312 = f32[1,2048,4,128]{1,3,2,0:T(8,128)} reshape(f32[8,256,4,128]{1,0,3,2:T(8,128)} %copy.66) | data formatting | bytes 8388608 | tf_op jit(solution)/shard_map/reshape | solution.py:70
  138.6 5.1 %fusion.8 = f32[4,2048,128]{2,1,0:T(8,128)S(1)} fusion(f32[1,2048,4,128]{1,3,2,0:T(8,128)} %reshape.312, bf16[1,128,4,64]{1,3,2,0:T(8,128)(2,1)S(1)} %copy-done.6), kind=kOutput, calls=%fused_computation.25 | convolution fusion | flops 805306368 | bytes 6356992 | tf_op jit(solution)/shard_map/qlhc,qkhc->qhlk/dot_general | solution.py:80
  143.7 1.6 fusion.61
  145.2 0.6 copy-done.3
  145.8 1.4 fusion.28
  147.2 1.8 convolution_convert_fusion.1
  149.0 3.8 fusion.2
  152.8 0.8 convolution_convert_fusion.2
  153.7 1.3 copy.92
  155.0 2.2 copy.70
  157.1 1.5 copy.93
  158.7 2.0 copy.71
  160.7 4.1 pad_maximum_fusion.1
  164.7 0.5 broadcast_in_dim.73
  165.2 3.3 scatter_fusion
  168.5 0.1 copy.72
  168.7 10.7 %copy.73 = bf16[2048,4,128]{2,1,0:T(4,128)(2,1)} copy(bf16[2048,4,128]{2,0,1:T(8,128)(2,1)S(1)} %bitcast.171) | data formatting | bytes 4194304 | tf_op jit(solution)/shard_map/reshape | solution.py:106
  179.4 4.4 %all-to-all-start = ((bf16[2048,4,128]{2,1,0:T(4,128)(2,1)}), bf16[2048,4,128]{2,1,0:T(4,128)(2,1)}, u32[]{:S(2)}, u32[]{:S(2)}) async-start(bf16[2048,4,128]{2,1,0:T(4,128)(2,1)} %copy.73), calls=%async_computation | async-start | bytes 4194304 | tf_op jit(solution)/shard_map/all_to_all | solution.py:105
  183.9 0.0 all-reduce.3.cloned.1.call-start
  183.9 2.7 fusion.58
  186.6 0.1 reduce_sum.59
  186.7 43.0 %all-reduce = (f32[1,8]{1,0:T(1,128)S(1)}, f32[1,8]{1,0:T(1,128)S(1)}) all-reduce(f32[1,8]{1,0:T(1,128)S(1)} %get-tuple-element.30, f32[1,8]{1,0:T(1,128)S(1)} %get-tuple-element.31), channel_id=1, replica_groups=mesh['enc'=4,'dec'=4,'ret'=2] {'enc','dec'}, use_global_device_ids=true, to_apply=%region_11.12 | all-reduce | flops 16 | bytes 128 | tf_op jit(solution)/shard_map/psum | solution.py:131
  229.7 0.6 reduce_max.19
  230.3 1.3 fusion.57
  231.5 1.3 fusion.54
  232.8 0.3 convolution_divide_fusion
  233.1 1.2 fusion.19
  234.3 3.0 fusion.23
  237.2 0.0 all-reduce.3.cloned.1.call-update
  237.3 0.0 reduce-scatter.2.cloned.1.call-start
  237.3 1.9 copy.74
  239.2 2.6 copy.76
  241.8 14.8 %convolution_convert_fusion = bf16[2048,4096]{1,0:T(8,128)(2,1)} fusion(bf16[512,2048]{0,1:T(8,128)(2,1)} %bitcast.176, bf16[512,4096]{1,0:T(8,128)(2,1)} %bitcast.182), kind=kOutput, calls=%fused_computation.6 | convolution fusion | flops 8598323200 | bytes 23068672 | tf_op jit(solution)/shard_map/dot_general | solution.py:151
  256.6 22.3 %copy.77 = bf16[4096,16,128]{2,1,0:T(8,128)(2,1)} copy(bf16[4096,16,128]{0,2,1:T(8,128)(2,1)} %bitcast.169) | data formatting | bytes 33554432 | tf_op jit(solution)/shard_map/convert_element_type | solution.py:159
  279.0 0.0 reduce-scatter.2.cloned.1.call-update
  279.0 11.8 %all-reduce.3.cloned.1.call-done = bf16[768,768]{0,1:T(8,128)(2,1)} async-done(((bf16[768,768]{0,1:T(8,128)(2,1)}), bf16[768,768]{0,1:T(8,128)(2,1)}) %all-reduce.3.cloned.1.call-update) | async-done | bytes 1179664 | tf_op jit(solution)/shard_map/psum | solution.py:149
  290.8 2.4 copy.79
  293.2 0.1 copy.75
  293.3 2.7 copy.78
  296.0 114.4 %reduce-scatter.2.cloned.1.call-done = bf16[512,16,128]{2,1,0:T(8,128)(2,1)} async-done(((bf16[4096,16,128]{2,1,0:T(8,128)(2,1)}), bf16[512,16,128]{2,1,0:T(8,128)(2,1)}) %reduce-scatter.2.cloned.1.call-update) | async-done | bytes 2097168 | tf_op jit(solution)/shard_map/reduce_scatter | solution.py:154
  (31 shorter events, 0.1 us)
Async XLA Ops:
  7.2 59.0 %copy-start = (bf16[768,768]{1,0:T(8,128)(2,1)S(1)}, bf16[768,768]{1,0:T(8,128)(2,1)}, u32[]{:S(2)}) copy-start(bf16[768,768]{1,0:T(8,128)(2,1)} %param.16) | copy-start | bytes 3538948
  57.6 7.6 %copy-start.9 = (s32[1,8]{1,0:T(1,128)S(1)}, s32[1,8]{1,0:T(1,128)}, u32[]{:S(2)}) copy-start(s32[1,8]{1,0:T(1,128)} %param.13) | copy-start | bytes 100
  57.6 7.6 %copy-start.2 = (s32[1,8]{1,0:T(1,128)S(1)}, s32[1,8]{1,0:T(1,128)}, u32[]{:S(2)}) copy-start(s32[1,8]{1,0:T(1,128)} %param.14) | copy-start | bytes 100
  57.6 8.5 %copy-start.7 = (f32[1,768]{1,0:T(1,128)S(1)}, f32[1,768]{1,0:T(1,128)}, u32[]{:S(2)}) copy-start(f32[1,768]{1,0:T(1,128)} %param.17) | copy-start | bytes 9220
  59.3 28.3 %collective-permute-start = (f32[512,4,128]{2,0,1:T(8,128)}, f32[512,4,128]{2,0,1:T(8,128)}, u32[]{:S(2)}, u32[]{:S(2)}) collective-permute-start(f32[512,4,128]{2,0,1:T(8,128)} %get-tuple-element.25), channel_id=1, source_target_pairs={{0,8},{8,16},{16,24},{24,0},{1,9},{9,17},{17,25},{25,1},{2,10},{10... | collective-permute-start | bytes 3145736 | tf_op jit(solution)/shard_map/ppermute | solution.py:63
  62.2 46.9 %collective-permute-start.1 = (f32[512,4,128]{2,0,1:T(8,128)}, f32[512,4,128]{2,0,1:T(8,128)}, u32[]{:S(2)}, u32[]{:S(2)}) collective-permute-start(f32[512,4,128]{2,0,1:T(8,128)} %get-tuple-element.24), channel_id=1, source_target_pairs={{0,16},{8,24},{16,0},{24,8},{1,17},{9,25},{17,1},{25,9},{2,18},{10... | collective-permute-start | bytes 3145736 | tf_op jit(solution)/shard_map/ppermute | solution.py:63
  63.7 45.7 %collective-permute-start.2 = (f32[512,4,128]{2,0,1:T(8,128)S(1)}, f32[512,4,128]{2,0,1:T(8,128)}, u32[]{:S(2)}, u32[]{:S(2)}) collective-permute-start(f32[512,4,128]{2,0,1:T(8,128)S(1)} %get-tuple-element.23), channel_id=1, source_target_pairs={{0,24},{8,0},{16,8},{24,16},{1,25},{9,1},{17,9},{25,17},{2,26},{10... | collective-permute-start | bytes 3145736 | tf_op jit(solution)/shard_map/ppermute | solution.py:63
  133.7 4.9 %copy-start.6 = (bf16[1,128,4,64]{1,3,2,0:T(8,128)(2,1)S(1)}, bf16[1,128,4,64]{1,3,2,0:T(8,128)(2,1)}, u32[]{:S(2)}) copy-start(bf16[1,128,4,64]{1,3,2,0:T(8,128)(2,1)} %param.11) | copy-start | bytes 196612
  143.6 2.2 copy-start.3
  143.6 2.2 copy-start.8
  145.2 3.8 copy-start.4
  179.4 57.9 %all-to-all-start = ((bf16[2048,4,128]{2,1,0:T(4,128)(2,1)}), bf16[2048,4,128]{2,1,0:T(4,128)(2,1)}, u32[]{:S(2)}, u32[]{:S(2)}) async-start(bf16[2048,4,128]{2,1,0:T(4,128)(2,1)} %copy.73), calls=%async_computation | async-start | bytes 4194304 | tf_op jit(solution)/shard_map/all_to_all | solution.py:105
  183.8 49.3 %copy-start.5 = (f32[2,256,768]{2,1,0:T(8,128)S(1)}, f32[2,256,768]{2,1,0:T(8,128)}, u32[]{:S(2)}) copy-start(f32[2,256,768]{2,1,0:T(8,128)} %get-tuple-element.29) | copy-start | bytes 4718596
  183.9 106.9 %all-reduce.3.cloned.1.call-start = ((), (), s32[]{:S(2)}) async-start(), calls=%async_computation.3 | async-start | bytes 2359296 | tf_op jit(solution)/shard_map/psum | solution.py:149
  237.3 173.2 %reduce-scatter.2.cloned.1.call-start = ((), (), s32[]{:S(2)}) async-start(), calls=%async_computation.2 | async-start | bytes 18874368 | tf_op jit(solution)/shard_map/reduce_scatter | solution.py:154
  293.3 117.1 %copy-start.1 = (bf16[768,768]{1,0:T(8,128)(2,1)S(1)}, bf16[768,768]{1,0:T(8,128)(2,1)}, u32[]{:S(2)}) copy-start(bf16[768,768]{1,0:T(8,128)(2,1)} %param.16) | copy-start | bytes 3538948
Sparse Core Ops, SparseCore 0:
  237.4 53.3 all-reduce.2
  294.9 115.4 reduce-scatter.1
